TPU v7x, 32 devices: a whole 2x2x4 slice. The times are simulated.
32 devices in a mesh: groups: 2 (over y), seq: 8 (over z, x), head: 1, sub: 2 (over core).
Axes of the slice: x: 2, y: 2, z: 4, core: 2. Of those that a mesh axis runs over, the one named last changes fastest.
Arguments:
- queries: bfloat16 [8192, 16, 128], P(('groups', 'seq'), ('head', 'sub')), parts along dimension 0, may hold values from -8 to 8
- key_rows: bfloat16 [8192, 16, 128], P(('groups', 'seq'), ('head', 'sub')), parts along dimension 0, may hold values from -8 to 8
- value_rows: bfloat16 [8192, 16, 128], P(('groups', 'seq'), ('head', 'sub')), parts along dimension 0, may hold values from -6 to 6
- grad_out: bfloat16 [8192, 16, 128], P(('groups', 'seq'), ('head', 'sub')), parts along dimension 0, may hold values from -6 to 6
- global_blocks: int32 [16], P('groups'), parts along dimension 0, may hold values from 0 to 15, as said below
Outputs:
- attended: bfloat16 [8192, 16, 128], P(('groups', 'seq'), ('head', 'sub')), parts along dimension 0
- grad_queries: bfloat16 [8192, 16, 128], P(('groups', 'seq'), ('head', 'sub')), parts along dimension 0
- grad_keys: bfloat16 [8192, 16, 128], P(('groups', 'seq'), ('head', 'sub')), parts along dimension 0
- grad_values: bfloat16 [8192, 16, 128], P(('groups', 'seq'), ('head', 'sub')), parts along dimension 0
There are 2 independent parts, one for each index of `groups`. A program takes and returns all parts, laid end to end along the dimension named above; each array names one. Nothing has to cross between parts.
Inputs may be any that keep to these rules, and one draw needn't show every extreme that they name: `global_blocks`: 8 different block indices in no fixed order; block 0 and block 15 are always among them.
All inputs are finite; a program needn't handle non-finite values.
Results may differ from a plain program's by a relative error of at most 0.025.
Values may be sent and summed in bfloat16 or wider, within the bound.
A program may use at most 256 MiB of HBM per device.

v0:
```python
import math
import jax
import jax.numpy as jnp
from jax import lax
from jax.sharding import PartitionSpec as P

BLOCK = 256


def shortened(array):

    def short(part):
        return part.astype(jnp.bfloat16) if part.dtype == jnp.float32 else part

    return jax.tree.map(short, array)


def from_partner(value, axis, bit):
    mask = 2**bit
    pairs = [(source, source ^ mask) for source in range(lax.axis_size(axis))]
    return lax.ppermute(value, axis, pairs)


def spread(array, axis, root):
    mine = lax.axis_index(axis) == root
    return lax.psum(jnp.where(mine, array, jnp.zeros_like(array)), axis)


def flip_pairs(array, bit_index):
    block_count = array.shape[0]
    stride = 1 << bit_index
    shaped = array.reshape((block_count // (2 * stride), 2, stride) + array.shape[1:])
    return jnp.flip(shaped, 1).reshape(array.shape)


def fetch_first(pair, bit_index):
    return jax.tree.map(
        lambda part, own: part.astype(own.dtype),
        from_partner(shortened(pair), "seq", bit_index),
        pair,
    )


def partner_stack(key_blocks, value_blocks, inner_bits, level_count, fetcher):
    key_list = [key_blocks]
    value_list = [value_blocks]
    for level_index in range(level_count):
        if level_index < inner_bits:
            key_list.append(flip_pairs(key_blocks, level_index))
            value_list.append(flip_pairs(value_blocks, level_index))
        else:
            far_keys, far_values = fetcher((key_blocks, value_blocks), level_index - inner_bits)
            key_list.append(far_keys)
            value_list.append(far_values)
    return (jnp.stack(key_list, 1), jnp.stack(value_list, 1))


def group_logits(query_group, key_group, global_keys, keep_group, scaling):
    near_part = jnp.einsum(
        "gqhd,glkhd->ghqlk", query_group, key_group, preferred_element_type=jnp.float32
    )
    far_part = jnp.einsum(
        "gqhd,nkhd->ghqnk", query_group, global_keys, preferred_element_type=jnp.float32
    )
    far_part = jnp.where(keep_group[:, None, None, :, None], far_part * scaling, -jnp.inf)
    lead_shape = near_part.shape[:3]
    return jnp.concatenate(
        [near_part.reshape(lead_shape + (-1,)) * scaling, far_part.reshape(lead_shape + (-1,))], -1
    )


def split_keys(array, slot_count, block_rows):
    lead_shape = array.shape[:3]
    near_part = array[..., : slot_count * block_rows].reshape(lead_shape + (slot_count, block_rows))
    far_part = array[..., slot_count * block_rows :].reshape(lead_shape + (-1, block_rows))
    return (near_part, far_part)


def on_device(queries, key_rows, value_rows, grad_out, global_blocks):
    row_count, head_count, head_width = queries.shape
    block_count = row_count // BLOCK
    seq_count = lax.axis_size("seq")
    total_blocks = block_count * seq_count
    level_count = total_blocks.bit_length() - 1
    inner_bits = block_count.bit_length() - 1
    slot_count = 1 + level_count
    global_count = global_blocks.shape[0]
    scaling = 1.0 / math.sqrt(head_width)
    first_block = lax.axis_index("seq") * block_count
    block_shape = (block_count, BLOCK, head_count, head_width)
    query_blocks = queries.reshape(block_shape)
    key_blocks = key_rows.reshape(block_shape)
    value_blocks = value_rows.reshape(block_shape)
    grad_blocks = grad_out.reshape(block_shape)
    block_ids = first_block + jnp.arange(block_count, dtype=jnp.int32)
    xor_offsets = jnp.bitwise_xor(global_blocks[None, :], block_ids[:, None])
    keep_global = jnp.bitwise_and(xor_offsets, xor_offsets - 1) != 0
    picked_keys = []
    picked_values = []
    for member in range(global_count):
        target = global_blocks[member]
        local_index = target % block_count
        key_single = lax.dynamic_index_in_dim(key_blocks, local_index, 0, keepdims=False)
        value_single = lax.dynamic_index_in_dim(value_blocks, local_index, 0, keepdims=False)
        key_got, value_got = (
            spread(key_single, "seq", target // block_count),
            spread(value_single, "seq", target // block_count),
        )
        picked_keys.append(key_got)
        picked_values.append(value_got)
    global_keys = jnp.stack(picked_keys, 0)
    global_values = jnp.stack(picked_values, 0)
    key_stack, value_stack = partner_stack(
        key_blocks, value_blocks, inner_bits, level_count, fetch_first
    )
    pair_count = block_count // 2

    def grouped(array):
        return array.reshape((pair_count, 2) + array.shape[1:])

    def forward_group(operands):
        query_group, key_group, value_group, keep_group = operands
        logits = group_logits(query_group, key_group, global_keys, keep_group, scaling)
        row_peak = jnp.max(logits, -1, keepdims=True)
        log_total = row_peak + jnp.log(jnp.sum(jnp.exp(logits - row_peak), -1, keepdims=True))
        weights = jnp.exp(logits - log_total).astype(jnp.bfloat16)
        near_weights, far_weights = split_keys(weights, slot_count, BLOCK)
        output = jnp.einsum(
            "ghqlk,glkhd->gqhd", near_weights, value_group, preferred_element_type=jnp.float32
        )
        output = output + jnp.einsum(
            "ghqnk,nkhd->gqhd", far_weights, global_values, preferred_element_type=jnp.float32
        )
        return (output.astype(jnp.bfloat16), log_total)

    attended_groups, log_totals = lax.map(
        forward_group,
        (grouped(query_blocks), grouped(key_stack), grouped(value_stack), grouped(keep_global)),
    )

    def backward_group(carried, operands):
        key_sum_now, value_sum_now = carried
        query_group, key_group, value_group, keep_group, grad_group, output_group, total_group = (
            operands
        )
        logits = group_logits(query_group, key_group, global_keys, keep_group, scaling)
        weights = jnp.exp(logits - total_group)
        weights_low = weights.astype(jnp.bfloat16)
        row_delta = jnp.sum(
            grad_group.astype(jnp.float32) * output_group.astype(jnp.float32), -1
        ).transpose(0, 2, 1)
        near_grad = jnp.einsum(
            "gqhd,glkhd->ghqlk", grad_group, value_group, preferred_element_type=jnp.float32
        )
        far_grad = jnp.einsum(
            "gqhd,nkhd->ghqnk", grad_group, global_values, preferred_element_type=jnp.float32
        )
        lead_shape = near_grad.shape[:3]
        grad_weights = jnp.concatenate(
            [near_grad.reshape(lead_shape + (-1,)), far_grad.reshape(lead_shape + (-1,))], -1
        )
        grad_logits = (weights * (grad_weights - row_delta[..., None]) * scaling).astype(
            jnp.bfloat16
        )
        near_logit, far_logit = split_keys(grad_logits, slot_count, BLOCK)
        near_weight, far_weight = split_keys(weights_low, slot_count, BLOCK)
        grad_query = jnp.einsum(
            "ghqlk,glkhd->gqhd", near_logit, key_group, preferred_element_type=jnp.float32
        )
        grad_query = grad_query + jnp.einsum(
            "ghqnk,nkhd->gqhd", far_logit, global_keys, preferred_element_type=jnp.float32
        )
        key_terms = jnp.einsum(
            "ghqlk,gqhd->glkhd", near_logit, query_group, preferred_element_type=jnp.float32
        )
        value_terms = jnp.einsum(
            "ghqlk,gqhd->glkhd", near_weight, grad_group, preferred_element_type=jnp.float32
        )
        key_sum_now = key_sum_now + jnp.einsum(
            "ghqnk,gqhd->nkhd", far_logit, query_group, preferred_element_type=jnp.float32
        )
        value_sum_now = value_sum_now + jnp.einsum(
            "ghqnk,gqhd->nkhd", far_weight, grad_group, preferred_element_type=jnp.float32
        )
        return (
            (key_sum_now, value_sum_now),
            (grad_query.astype(jnp.bfloat16), key_terms, value_terms),
        )

    global_zeros = jnp.zeros((global_count, BLOCK, head_count, head_width), jnp.float32)
    global_terms, back_outputs = lax.scan(
        backward_group,
        (global_zeros, global_zeros),
        (
            grouped(query_blocks),
            grouped(key_stack),
            grouped(value_stack),
            grouped(keep_global),
            grouped(grad_blocks),
            attended_groups,
            log_totals,
        ),
    )
    grad_query_groups, key_term_groups, value_term_groups = back_outputs
    slot_shape = (block_count, slot_count, BLOCK, head_count, head_width)
    key_terms_all = key_term_groups.reshape(slot_shape)
    value_terms_all = value_term_groups.reshape(slot_shape)
    grad_key_sum = key_terms_all[:, 0]
    grad_value_sum = value_terms_all[:, 0]
    for level_index in range(level_count):
        key_term = key_terms_all[:, 1 + level_index]
        value_term = value_terms_all[:, 1 + level_index]
        if level_index < inner_bits:
            grad_key_sum = grad_key_sum + flip_pairs(key_term, level_index)
            grad_value_sum = grad_value_sum + flip_pairs(value_term, level_index)
        else:
            back_key, back_value = from_partner(
                (key_term.astype(jnp.bfloat16), value_term.astype(jnp.bfloat16)),
                "seq",
                level_index - inner_bits,
            )
            grad_key_sum = grad_key_sum + back_key.astype(jnp.float32)
            grad_value_sum = grad_value_sum + back_value.astype(jnp.float32)
    key_partial = global_terms[0].astype(jnp.bfloat16).astype(jnp.float32)
    value_partial = global_terms[1].astype(jnp.bfloat16).astype(jnp.float32)
    key_share, value_share = (
        lax.psum_scatter(
            key_partial.astype(jnp.bfloat16), "seq", scatter_dimension=1, tiled=True
        ).astype(jnp.float32),
        lax.psum_scatter(
            value_partial.astype(jnp.bfloat16), "seq", scatter_dimension=1, tiled=True
        ).astype(jnp.float32),
    )
    every_block = jnp.arange(total_blocks, dtype=jnp.int32)
    route_weight = (
        (global_blocks[:, None] == every_block[None, :])
        .astype(jnp.float32)
        .T[:, :, None, None, None]
    )
    key_send = jnp.sum(route_weight * key_share[None], 1)
    value_send = jnp.sum(route_weight * value_share[None], 1)
    key_owned, value_owned = (
        lax.all_to_all(
            key_send.astype(jnp.bfloat16), "seq", split_axis=0, concat_axis=1, tiled=True
        ).astype(key_send.dtype),
        lax.all_to_all(
            value_send.astype(jnp.bfloat16), "seq", split_axis=0, concat_axis=1, tiled=True
        ).astype(value_send.dtype),
    )
    grad_key_sum = grad_key_sum + key_owned
    grad_value_sum = grad_value_sum + value_owned
    return (
        attended_groups.reshape(queries.shape),
        grad_query_groups.reshape(queries.shape),
        grad_key_sum.astype(jnp.bfloat16).reshape(queries.shape),
        grad_value_sum.astype(jnp.bfloat16).reshape(queries.shape),
    )


def solution(mesh):
    in_specs = (
        P(("groups", "seq"), ("head", "sub"), None),
        P(("groups", "seq"), ("head", "sub"), None),
        P(("groups", "seq"), ("head", "sub"), None),
        P(("groups", "seq"), ("head", "sub"), None),
        P("groups"),
    )
    out_specs = (
        P(("groups", "seq"), ("head", "sub"), None),
        P(("groups", "seq"), ("head", "sub"), None),
        P(("groups", "seq"), ("head", "sub"), None),
        P(("groups", "seq"), ("head", "sub"), None),
    )
    return jax.shard_map(
        on_device, mesh=mesh, in_specs=in_specs, out_specs=out_specs, check_vma=False
    )
```

profile of v0, /device:TPU:0, one launch (start us, length us, event | category | flops | bytes accessed | tf_op | source)
XLA Modules:
  0.0 989.2 jit_solution(14491541534180600365)
XLA Ops:
  59.7 26.8 %collective-permute-done.3 = bf16[2,256,8,128]{3,1,2,0:T(8,128)(2,1)} collective-permute-done((bf16[2,256,8,128]{3,1,2,0:T(8,128)(2,1)}, bf16[2,256,8,128]{3,1,2,0:T(8,128)(2,1)}, u32[]{:S(2)}, u32[]{:S(2)}) %collective-permute-start.3) | collective-permute-done | bytes 1048608 | tf_op jit(solution)/shard_map/ppermute | solution.py:21
  91.0 45.2 %collective-permute-done.4 = bf16[2,256,8,128]{3,1,2,0:T(8,128)(2,1)} collective-permute-done((bf16[2,256,8,128]{3,1,2,0:T(8,128)(2,1)}, bf16[2,256,8,128]{3,1,2,0:T(8,128)(2,1)}, u32[]{:S(2)}, u32[]{:S(2)}) %collective-permute-start.4) | collective-permute-done | bytes 1048608 | tf_op jit(solution)/shard_map/ppermute | solution.py:21
  143.4 80.7 %collective-permute-done.1 = bf16[2,256,8,128]{1,3,2,0:T(8,128)(2,1)} collective-permute-done((bf16[2,256,8,128]{1,3,2,0:T(8,128)(2,1)}, bf16[2,256,8,128]{1,3,2,0:T(8,128)(2,1)}, u32[]{:S(2)}, u32[]{:S(2)}) %collective-permute-start.1) | collective-permute-done | bytes 1048608 | tf_op jit(solution)/shard_map/ppermute | solution.py:21
  228.8 8.7 fusion.42
  237.5 8.6 fusion.33
  246.1 166.9 %all-reduce.3.cloned.1.call-done = (bf16[1,256,8,128]{3,1,0,2:T(8,128)(2,1)}, bf16[1,256,8,128]{3,1,0,2:T(8,128)(2,1)}, bf16[1,256,8,128]{3,1,0,2:T(8,128)(2,1)}...) async-done(((bf16[1,256,8,128]{3,1,0,2:T(8,128)(2,1)}, ...) | async-done | bytes 8388624 | tf_op jit(solution)/shard_map/psum | solution.py:26
  418.9 13.2 %fusion.43 = (f32[2,8,256]{2,0,1:T(2,128)S(1)}, f32[2,8,256,8,256]{2,4,0,3,1:T(8,128)}) fusion(bf16[2,256,8,128,1]{3,2,1,0,4:T(8,128)(2,1)S(1)} %bitcast.232, bf16[8,256,8,128]{3,1,0,2:T(8,128)(2,1)S(1)} %constant_dynamic-update-slice_fusion.1, pred[2,8]{0,1:T(8,128)(4,1)S(1)} %fusion.40), kind=kOutput, calls=%fused_computation.134 | convolution fusion | flops 2172645376 | bytes 38813712 | tf_op jit(solution)/shard_map/while/body/eval_jaxpr/gqhd,nkhd->ghqnk/dot_general | solution.py:62
  432.1 22.8 %copy.255 = f32[2,8,256,8,256]{2,4,3,1,0:T(8,128)} copy(f32[2,8,256,8,256]{2,4,0,3,1:T(8,128)} %get-tuple-element.127) | data formatting | bytes 67108864 | tf_op jit(solution)/shard_map/while/body/eval_jaxpr/jit(_where)/select_n | solution.py:65
  454.9 17.3 %exponential_reduce_fusion = f32[2,8,256]{2,1,0:T(8,128)S(1)} fusion(f32[2,8,256,2048]{2,3,1,0:T(8,128)} %bitcast.235, f32[2,8,256,1280]{2,3,1,0:T(8,128)} %bitcast.238, f32[2,8,256]{2,1,0:T(8,128)S(1)} %copy_maximum_fusion), kind=kLoop, calls=%fused_computation.6 | loop fusion | flops 40890368 | bytes 54558720 | tf_op jit(solution)/shard_map/while/body/eval_jaxpr/reduce_sum | solution.py:125
  472.2 27.0 %fusion.3 = bf16[2,8,256,3328]{2,3,1,0:T(8,128)(2,1)} fusion(f32[2,8,256,2048]{2,3,1,0:T(8,128)} %bitcast.236, f32[2,8,256,1280]{2,3,1,0:T(8,128)} %bitcast.239, f32[2,8,256]{2,1,0:T(8,128)S(1)} %log_add_fusion), kind=kLoop, calls=%fused_computation.7 | loop fusion | flops 40894464 | bytes 81805312 | tf_op jit(solution)/shard_map/while/body/eval_jaxpr/convert_element_type | solution.py:126
  499.2 14.0 %slice.103 = bf16[2,8,256,2048]{2,3,1,0:T(8,128)(2,1)} slice(bf16[2,8,256,3328]{2,3,1,0:T(8,128)(2,1)} %fusion.3), slice={[0:2], [0:8], [0:256], [1280:3328]} | slice | bytes 33554432 | tf_op jit(solution)/shard_map/while/body/eval_jaxpr/slice | solution.py:75
  513.3 8.9 slice.102
  532.7 17.9 %convolution_bitcast_fusion = f32[2,8,256,8,256]{2,4,0,3,1:T(8,128)} fusion(bf16[8,256,8,128]{3,1,0,2:T(8,128)(2,1)} %constant_dynamic-update-slice_fusion.9, bf16[2,256,8,128,1]{3,2,1,0,4:T(8,128)(2,1)S(1)} %bitcast.262), kind=kOutput, calls=%fused_computation.11 | convolution fusion | flops 2147483648 | bytes 38797312 | tf_op jit(solution)/shard_map/while/body/eval_jaxpr/gqhd,nkhd->ghqnk/dot_general | solution.py:155
  550.7 9.8 fusion.8
  568.1 22.8 %copy.272 = f32[2,8,256,8,256]{2,4,3,1,0:T(8,128)} copy(f32[2,8,256,8,256]{2,4,0,3,1:T(8,128)} %convolution_bitcast_fusion) | data formatting | bytes 67108864 | tf_op jit(solution)/shard_map/while/body/eval_jaxpr/gqhd,nkhd->ghqnk/transpose | solution.py:155
  590.9 43.7 %fusion.2 = bf16[2,8,256,3328]{2,3,1,0:T(8,128)(2,1)} fusion(f32[2,8,256,2048]{2,3,1,0:T(8,128)} %bitcast.243, f32[2,8,256,1280]{2,3,1,0:T(8,128)} %bitcast.248, f32[2,8,256,2048]{2,3,1,0:T(8,128)} %bitcast.237, f32[2,8,256,1280]{2,3,1,0:T(8,128)} %bitcast.240, f32[2,8,256]{2,1,0:T(8,128)S(1)} %bitcast.272, f32[2,8,256]{2,1,0:T(8,128)S(1)} %log_add_fusion), kind=kLoop, calls=%fused_computation.4 | loop fusion | flops 95420416 | bytes 136347648 | tf_op jit(solution)/shard_map/while/body/eval_jaxpr/convert_element_type | solution.py:162
  634.7 13.8 %slice.105 = bf16[2,8,256,2048]{2,3,1,0:T(8,128)(2,1)} slice(bf16[2,8,256,3328]{2,3,1,0:T(8,128)(2,1)} %fusion.2), slice={[0:2], [0:8], [0:256], [1280:3328]} | slice | bytes 33554432 | tf_op jit(solution)/shard_map/while/body/eval_jaxpr/slice | solution.py:75
  648.5 12.2 %fusion.35 = bf16[8,8,256,128,1]{3,2,1,0,4:T(8,128)(2,1)} fusion(bf16[2,8,256,8,256]{2,4,3,1,0:T(8,128)(2,1)} %bitcast.249, bf16[2,256,8,128,1]{3,2,1,0,4:T(8,128)(2,1)S(1)} %bitcast.233), kind=kOutput, calls=%fused_computation.72 | convolution fusion | flops 2147483648 | bytes 22020096 | tf_op jit(solution)/shard_map/while/body/eval_jaxpr/ghqnk,gqhd->nkhd/dot_general | solution.py:179
  660.7 4.6 copy.415
  665.4 12.4 %fusion.30 = bf16[8,8,256,128,1]{3,2,1,0,4:T(8,128)(2,1)} fusion(bf16[2,8,256,8,256]{2,4,3,1,0:T(8,128)(2,1)} %bitcast.252, bf16[2,256,8,128,1]{3,2,1,0,4:T(8,128)(2,1)S(1)} %bitcast.263), kind=kOutput, calls=%fused_computation.67 | convolution fusion | flops 2147483648 | bytes 22020096 | tf_op jit(solution)/shard_map/while/body/eval_jaxpr/ghqnk,gqhd->nkhd/dot_general | solution.py:182
  677.7 4.6 copy.416
  682.4 9.0 slice.104
  691.4 12.8 %fusion.45 = (bf16[2,5,256,8,128]{4,2,1,3,0:T(8,128)(2,1)}, f32[2,5,256,8,128]{4,2,1,3,0:T(8,128)}) fusion(bf16[2,8,256,5,256]{2,4,3,1,0:T(8,128)(2,1)} %bitcast.244, bf16[2,256,8,128,1]{3,2,1,0,4:T(8,128)(2,1)S(1)} %bitcast.264), kind=kOutput, calls=%fused_computation.136 | convolution fusion | flops 1344798720 | bytes 27262976 | tf_op jit(solution)/shard_map/while/body/eval_jaxpr/ghqlk,gqhd->glkhd/dot_general | solution.py:176
  710.6 7.3 fusion.44
  717.9 56.3 %reduce-scatter.3.cloned.1.call-done = bf16[8,32,8,128]{3,1,2,0:T(8,128)(2,1)} async-done(((bf16[8,256,8,128]{3,1,2,0:T(8,128)(2,1)}), bf16[8,32,8,128]{3,1,2,0:T(8,128)(2,1)}) %reduce-scatter.3.cloned.1.call-update) | async-done | bytes 524304 | tf_op jit(solution)/shard_map/reduce_scatter | solution.py:227
  775.4 91.1 %reduce-scatter.5.cloned.1.call-done = bf16[8,32,8,128]{3,1,2,0:T(8,128)(2,1)} async-done(((bf16[8,256,8,128]{3,1,2,0:T(8,128)(2,1)}), bf16[8,32,8,128]{3,1,2,0:T(8,128)(2,1)}) %reduce-scatter.5.cloned.1.call-update) | async-done | bytes 524304 | tf_op jit(solution)/shard_map/reduce_scatter | solution.py:230
  883.3 8.5 fusion.10
  891.8 10.5 %all-to-all-done.1 = bf16[16,32,8,128]{3,2,1,0:T(8,128)(2,1)} async-done(((bf16[16,32,8,128]{3,2,1,0:T(8,128)(2,1)}), bf16[16,32,8,128]{3,2,1,0:T(8,128)(2,1)}, u32[]{:S(2)}, u32[]{:S(2)}) %all-to-all-start.1) | async-done | bytes 1048608 | tf_op jit(solution)/shard_map/all_to_all | solution.py:246
  902.3 4.5 all-to-all-start
  906.7 8.4 fusion.26
  932.4 8.0 all-to-all-done
  942.3 35.2 %collective-permute-done.8 = bf16[2,256,8,128]{3,1,2,0:T(8,128)(2,1)} collective-permute-done((bf16[2,256,8,128]{3,1,2,0:T(8,128)(2,1)}, bf16[2,256,8,128]{3,1,2,0:T(8,128)(2,1)}, u32[]{:S(2)}, u32[]{:S(2)}) %collective-permute-start.8) | collective-permute-done | bytes 1048608 | tf_op jit(solution)/shard_map/ppermute | solution.py:21
  (145 shorter events, 121.2 us)
Async XLA Ops:
  7.2 221.6 %copy-start = (bf16[512,8,128]{2,1,0:T(8,128)(2,1)S(1)}, bf16[512,8,128]{2,1,0:T(8,128)(2,1)}, u32[]{:S(2)}) copy-start(bf16[512,8,128]{2,1,0:T(8,128)(2,1)} %param.5) | copy-start | bytes 3145732
  7.2 24.6 %copy-start.4 = (bf16[512,8,128]{2,1,0:T(8,128)(2,1)S(1)}, bf16[512,8,128]{2,1,0:T(8,128)(2,1)}, u32[]{:S(2)}) copy-start(bf16[512,8,128]{2,1,0:T(8,128)(2,1)} %param.6) | copy-start | bytes 3145732
  7.2 405.8 %all-reduce.3.cloned.1.call-start = ((), (), s32[]{:S(2)}) async-start(), calls=%async_computation.6 | async-start | bytes 16777216 | tf_op jit(solution)/shard_map/psum | solution.py:26
  41.4 732.8 %reduce-scatter.3.cloned.1.call-start = ((), (), s32[]{:S(2)}) async-start(), calls=%async_computation.4 | async-start | bytes 4718592 | tf_op jit(solution)/shard_map/reduce_scatter | solution.py:227
  42.8 43.7 %collective-permute-start.3 = (bf16[2,256,8,128]{3,1,2,0:T(8,128)(2,1)}, bf16[2,256,8,128]{3,1,2,0:T(8,128)(2,1)}, u32[]{:S(2)}, u32[]{:S(2)}) collective-permute-start(bf16[2,256,8,128]{3,1,2,0:T(8,128)(2,1)} %copy.241), channel_id=1, source_target_pairs={{0,2},{2,0},{4,6},{6,4},{8,10},{10,8},{12,14},{14,12},{1,3},{3,1},... | collective-permute-start | bytes 3145736 | tf_op jit(solution)/shard_map/ppermute | solution.py:21
  45.7 90.5 %collective-permute-start.4 = (bf16[2,256,8,128]{3,1,2,0:T(8,128)(2,1)}, bf16[2,256,8,128]{3,1,2,0:T(8,128)(2,1)}, u32[]{:S(2)}, u32[]{:S(2)}) collective-permute-start(bf16[2,256,8,128]{3,1,2,0:T(8,128)(2,1)} %copy.241), channel_id=1, source_target_pairs={{0,4},{2,6},{4,0},{6,2},{8,12},{10,14},{12,8},{14,10},{1,5},{3,7},... | collective-permute-start | bytes 3145736 | tf_op jit(solution)/shard_map/ppermute | solution.py:21
  47.3 92.5 %collective-permute-start.5 = (bf16[2,256,8,128]{3,1,2,0:T(8,128)(2,1)}, bf16[2,256,8,128]{3,1,2,0:T(8,128)(2,1)}, u32[]{:S(2)}, u32[]{:S(2)}) collective-permute-start(bf16[2,256,8,128]{3,1,2,0:T(8,128)(2,1)} %copy.241), channel_id=1, source_target_pairs={{0,8},{2,10},{4,12},{6,14},{8,0},{10,2},{12,4},{14,6},{1,9},{3,11}... | collective-permute-start | bytes 3145736 | tf_op jit(solution)/shard_map/ppermute | solution.py:21
  51.4 89.8 %collective-permute-start = (bf16[2,256,8,128]{1,3,2,0:T(8,128)(2,1)}, bf16[2,256,8,128]{1,3,2,0:T(8,128)(2,1)}, u32[]{:S(2)}, u32[]{:S(2)}) collective-permute-start(bf16[2,256,8,128]{1,3,2,0:T(8,128)(2,1)} %copy.236), channel_id=1, source_target_pairs={{0,2},{2,0},{4,6},{6,4},{8,10},{10,8},{12,14},{14,12},{1,3},{3,1},... | collective-permute-start | bytes 3145736 | tf_op jit(solution)/shard_map/ppermute | solution.py:21
  51.9 172.2 %collective-permute-start.1 = (bf16[2,256,8,128]{1,3,2,0:T(8,128)(2,1)}, bf16[2,256,8,128]{1,3,2,0:T(8,128)(2,1)}, u32[]{:S(2)}, u32[]{:S(2)}) collective-permute-start(bf16[2,256,8,128]{1,3,2,0:T(8,128)(2,1)} %copy.236), channel_id=1, source_target_pairs={{0,4},{2,6},{4,0},{6,2},{8,12},{10,14},{12,8},{14,10},{1,5},{3,7},... | collective-permute-start | bytes 3145736 | tf_op jit(solution)/shard_map/ppermute | solution.py:21
  56.5 30.0 %copy-start.11 = (bf16[2,256,8,128]{1,3,2,0:T(8,128)(2,1)S(1)}, bf16[2,256,8,128]{1,3,2,0:T(8,128)(2,1)}, u32[]{:S(2)}) copy-start(bf16[2,256,8,128]{1,3,2,0:T(8,128)(2,1)} %copy.236) | copy-start | bytes 3145732
  86.5 142.2 %collective-permute-start.2 = (bf16[2,256,8,128]{1,3,2,0:T(8,128)(2,1)S(1)}, bf16[2,256,8,128]{1,3,2,0:T(8,128)(2,1)S(1)}, u32[]{:S(2)}, u32[]{:S(2)}) collective-permute-start(bf16[2,256,8,128]{1,3,2,0:T(8,128)(2,1)S(1)} %copy-done.11), channel_id=1, source_target_pairs={{0,8},{2,10},{4,12},{6,14},{8,0},{10,2},{12,4},{14,6},{1,9},{3,11}... | collective-permute-start | bytes 3145736 | tf_op jit(solution)/shard_map/ppermute | solution.py:21
  141.2 96.2 %copy-start.2 = (bf16[2,5,256,8,128]{4,2,1,3,0:T(8,128)(2,1)}, bf16[2,5,256,8,128]{4,2,1,3,0:T(8,128)(2,1)S(1)}, u32[]{:S(2)}) copy-start(bf16[2,5,256,8,128]{4,2,1,3,0:T(8,128)(2,1)S(1)} %bitcast_dynamic-update-slice_fusion) | copy-start | bytes 15728644
  228.8 8.7 copy-start.5
  228.8 8.7 copy-start.8
  418.9 13.2 %copy-start.6 = (bf16[8,256,8,128]{3,1,0,2:T(8,128)(2,1)}, bf16[8,256,8,128]{3,1,0,2:T(8,128)(2,1)S(1)}, u32[]{:S(2)}) copy-start(bf16[8,256,8,128]{3,1,0,2:T(8,128)(2,1)S(1)} %constant_dynamic-update-slice_fusion.1) | copy-start | bytes 12582916
  513.2 15.0 %copy-start.16 = (bf16[1,256,8,128]{3,1,0,2:T(8,128)(2,1)S(1)}, bf16[1,256,8,128]{3,1,0,2:T(8,128)(2,1)}, u32[]{:S(2)}) copy-start(bf16[1,256,8,128]{3,1,0,2:T(8,128)(2,1)} %get-tuple-element.74) | copy-start | bytes 1572868
  513.3 15.9 %copy-start.15 = (bf16[1,256,8,128]{3,1,0,2:T(8,128)(2,1)S(1)}, bf16[1,256,8,128]{3,1,0,2:T(8,128)(2,1)}, u32[]{:S(2)}) copy-start(bf16[1,256,8,128]{3,1,0,2:T(8,128)(2,1)} %get-tuple-element.75) | copy-start | bytes 1572868
  522.2 8.8 copy-start.13
  522.2 9.7 copy-start.12
  532.7 27.8 %slice-start = ((s8[10485760]{0:T(1024)(128)(4,1)}), s8[2097152]{0:T(1024)(128)(4,1)S(1)}, s32[]{:S(2)}) async-start(s8[10485760]{0:T(1024)(128)(4,1)} %bitcast.245), calls=%async_computation.7 | async-start | bytes 4194304
  532.7 27.8 %slice-start.1 = ((s8[10485760]{0:T(1024)(128)(4,1)}), s8[4194304]{0:T(1024)(128)(4,1)S(1)}, s32[]{:S(2)}) async-start(s8[10485760]{0:T(1024)(128)(4,1)} %bitcast.245), calls=%async_computation.8 | async-start | bytes 8388608
  550.7 9.8 slice-start.2
  665.3 201.2 %reduce-scatter.5.cloned.1.call-start = ((), (), s32[]{:S(2)}) async-start(), calls=%async_computation.5 | async-start | bytes 4718592 | tf_op jit(solution)/shard_map/reduce_scatter | solution.py:230
  691.4 19.2 %copy-start.1 = (bf16[2,8,256,1280]{2,3,1,0:T(8,128)(2,1)S(1)}, bf16[2,8,256,1280]{2,3,1,0:T(8,128)(2,1)}, u32[]{:S(2)}) copy-start(bf16[2,8,256,1280]{2,3,1,0:T(8,128)(2,1)} %slice.104) | copy-start | bytes 31457284
  707.9 210.5 %collective-permute-start.10 = (bf16[2,256,8,128]{3,1,2,0:T(8,128)(2,1)}, bf16[2,256,8,128]{3,1,2,0:T(8,128)(2,1)}, u32[]{:S(2)}, u32[]{:S(2)}) collective-permute-start(bf16[2,256,8,128]{3,1,2,0:T(8,128)(2,1)} %get-tuple-element.96), channel_id=1, source_target_pairs={{0,4},{2,6},{4,0},{6,2},{8,12},{10,14},{12,8},{14,10},{1,5},{3,7},... | collective-permute-start | bytes 3145736 | tf_op jit(solution)/shard_map/ppermute | solution.py:21
  707.9 219.5 %collective-permute-start.11 = (bf16[2,256,8,128]{3,1,2,0:T(8,128)(2,1)}, bf16[2,256,8,128]{3,1,2,0:T(8,128)(2,1)}, u32[]{:S(2)}, u32[]{:S(2)}) collective-permute-start(bf16[2,256,8,128]{3,1,2,0:T(8,128)(2,1)} %get-tuple-element.80), channel_id=1, source_target_pairs={{0,8},{2,10},{4,12},{6,14},{8,0},{10,2},{12,4},{14,6},{1,9},{3,11}... | collective-permute-start | bytes 3145736 | tf_op jit(solution)/shard_map/ppermute | solution.py:21
  708.9 218.5 %collective-permute-start.9 = (bf16[2,256,8,128]{3,1,2,0:T(8,128)(2,1)}, bf16[2,256,8,128]{3,1,2,0:T(8,128)(2,1)}, u32[]{:S(2)}, u32[]{:S(2)}) collective-permute-start(bf16[2,256,8,128]{3,1,2,0:T(8,128)(2,1)} %get-tuple-element.79), channel_id=1, source_target_pairs={{0,2},{2,0},{4,6},{6,4},{8,10},{10,8},{12,14},{14,12},{1,3},{3,1},... | collective-permute-start | bytes 3145736 | tf_op jit(solution)/shard_map/ppermute | solution.py:21
  871.7 30.6 %all-to-all-start.1 = ((bf16[16,32,8,128]{3,2,1,0:T(8,128)(2,1)}), bf16[16,32,8,128]{3,2,1,0:T(8,128)(2,1)}, u32[]{:S(2)}, u32[]{:S(2)}) async-start(bf16[16,32,8,128]{3,2,1,0:T(8,128)(2,1)} %get-tuple-element.46), calls=%async_computation.3 | async-start | bytes 2097152 | tf_op jit(solution)/shard_map/all_to_all | solution.py:246
  879.8 62.5 %collective-permute-start.6 = (bf16[2,256,8,128]{3,1,2,0:T(8,128)(2,1)}, bf16[2,256,8,128]{3,1,2,0:T(8,128)(2,1)}, u32[]{:S(2)}, u32[]{:S(2)}) collective-permute-start(bf16[2,256,8,128]{3,1,2,0:T(8,128)(2,1)} %get-tuple-element.97), channel_id=1, source_target_pairs={{0,2},{2,0},{4,6},{6,4},{8,10},{10,8},{12,14},{14,12},{1,3},{3,1},... | collective-permute-start | bytes 3145736 | tf_op jit(solution)/shard_map/ppermute | solution.py:21
  881.8 60.5 %collective-permute-start.7 = (bf16[2,256,8,128]{3,1,2,0:T(8,128)(2,1)}, bf16[2,256,8,128]{3,1,2,0:T(8,128)(2,1)}, u32[]{:S(2)}, u32[]{:S(2)}) collective-permute-start(bf16[2,256,8,128]{3,1,2,0:T(8,128)(2,1)} %get-tuple-element.99), channel_id=1, source_target_pairs={{0,4},{2,6},{4,0},{6,2},{8,12},{10,14},{12,8},{14,10},{1,5},{3,7},... | collective-permute-start | bytes 3145736 | tf_op jit(solution)/shard_map/ppermute | solution.py:21
  902.3 38.2 %all-to-all-start = ((bf16[16,32,8,128]{3,2,1,0:T(8,128)(2,1)}), bf16[16,32,8,128]{3,2,1,0:T(8,128)(2,1)}, u32[]{:S(2)}, u32[]{:S(2)}) async-start(bf16[16,32,8,128]{3,2,1,0:T(8,128)(2,1)} %get-tuple-element.47), calls=%async_computation.1 | async-start | bytes 2097152 | tf_op jit(solution)/shard_map/all_to_all | solution.py:243
  918.4 59.2 %collective-permute-start.8 = (bf16[2,256,8,128]{3,1,2,0:T(8,128)(2,1)}, bf16[2,256,8,128]{3,1,2,0:T(8,128)(2,1)}, u32[]{:S(2)}, u32[]{:S(2)}) collective-permute-start(bf16[2,256,8,128]{3,1,2,0:T(8,128)(2,1)} %get-tuple-element.98), channel_id=1, source_target_pairs={{0,8},{2,10},{4,12},{6,14},{8,0},{10,2},{12,4},{14,6},{1,9},{3,11}... | collective-permute-start | bytes 3145736 | tf_op jit(solution)/shard_map/ppermute | solution.py:21
  (10 other events, 55.3 us)
Sparse Core Ops, SparseCore 0:
  41.5 371.4 all-reduce.2
  665.4 108.7 reduce-scatter.2
  777.9 88.5 reduce-scatter.4
where the time goes:
time: 994 us; the launch traced here: 989 us
  waiting for transfers between devices  526 us (53%)
  local copies, waits for them, and re-layouts  162 us (16%)
  matrix products  124 us (12%)
  other arithmetic  113 us (11%)
  between operations  34.6 us (3%)
  starting transfers between devices  29.4 us (3%)
    ppermute x12, waiting for transfers between devices, from_partner(): return lax.ppermute(value, axis, pairs)  193 us
    psum x1, waiting for transfers between devices, spread(): return lax.psum(jnp.where(mine, array, jnp.zeros_like(array)), axis)  167 us
    reduce_scatter x1, waiting for transfers between devices, on_device(): lax.psum_scatter(value_partial.astype(jnp.bfloat16), 'seq', scatter_dimen...  91.1 us
    reduce_scatter x1, waiting for transfers between devices, on_device(): lax.psum_scatter(key_partial.astype(jnp.bfloat16), 'seq', scatter_dimensi...  56.3 us
    convert_element_type x1, other arithmetic, backward_group(): (weights * (grad_weights - row_delta[..., None]) * scaling).astype(jnp.bf...  43.7 us
    unnamed x74, local copies, waits for them, and re-layouts  30 us
    slice x2, local copies, waits for them, and re-layouts, split_keys(): array[..., slot_count * block_rows:].reshape(lead_shape + (-1, block_rows))  27.8 us
    convert_element_type x1, other arithmetic, forward_group(): weights = jnp.exp(logits - log_total).astype(jnp.bfloat16)  27 us
  transfers between devices with their start and end apart: 17, of which 11 were waited for; matrix products, arithmetic and copies ran while one was open for 13% of the time, Pallas kernels for 0%

commit v1 on v0

--- a/solution.py
+++ b/solution.py
@@ -23,7 +23,7 @@
 
 def spread(array, axis, root):
     mine = lax.axis_index(axis) == root
-    return lax.psum(jnp.where(mine, array, jnp.zeros_like(array)), axis)
+    return jnp.sum(lax.all_gather(jnp.where(mine, array, jnp.zeros_like(array)), axis), axis=0)
 
 
 def flip_pairs(array, bit_index):

time: 994 us -> 1760 us (1.77)
  waiting for transfers between devices: 526 us -> 1230 us
  other arithmetic: 113 us -> 159 us
    all_gather x0 -> x16, waiting for transfers between devices: none -> 905 us  [spread(): lax.all_gather(jnp.where(mine, array, jnp.zeros_like(array)), axis)]
    psum x1 -> x0, waiting for transfers between devices: 167 us -> none  [spread(): return lax.psum(jnp.where(mine, array, jnp.zeros_like(array)), axis)]
    reduce_sum x0 -> x16, other arithmetic: none -> 49.4 us  [spread(): jnp.sum(lax.all_gather(jnp.where(mine, array, jnp.zeros_like(array)), axi...]
    ppermute x12, waiting for transfers between devices: 193 us -> 152 us  [from_partner(): return lax.ppermute(value, axis, pairs)]
  transfers between devices with their start and end apart: 17 -> 32, of which waited for: 11 -> 22; matrix products, arithmetic and copies ran while one was open for 13% -> 17% of each run, Pallas kernels for 0% -> 0%
where the time goes in v1:
time: 1760 us
  waiting for transfers between devices  1230 us (70%)
  local copies, waits for them, and re-layouts  173 us (10%)
  other arithmetic  159 us (9%)
  matrix products  129 us (7%)
  between operations  35.9 us (2%)
  starting transfers between devices  29.3 us (2%)
    all_gather x16, waiting for transfers between devices, spread(): lax.all_gather(jnp.where(mine, array, jnp.zeros_like(array)), axis)  905 us
    ppermute x12, waiting for transfers between devices, from_partner(): return lax.ppermute(value, axis, pairs)  152 us
    reduce_scatter x1, waiting for transfers between devices, on_device(): lax.psum_scatter(value_partial.astype(jnp.bfloat16), 'seq', scatter_dimen...  91.3 us
    reduce_scatter x1, waiting for transfers between devices, on_device(): lax.psum_scatter(key_partial.astype(jnp.bfloat16), 'seq', scatter_dimensi...  55.3 us
    reduce_sum x16, other arithmetic, spread(): jnp.sum(lax.all_gather(jnp.where(mine, array, jnp.zeros_like(array)), axi...  49.4 us
    convert_element_type x1, other arithmetic, backward_group(): (weights * (grad_weights - row_delta[..., None]) * scaling).astype(jnp.bf...  43.4 us
  transfers between devices with their start and end apart: 32, of which 22 were waited for; matrix products, arithmetic and copies ran while one was open for 17% of the time, Pallas kernels for 0%

profile of v1, /device:TPU:0, one launch (start us, length us, event | category | flops | bytes accessed | tf_op | source)
XLA Modules:
  0.0 1756.2 jit_solution(17307997905410995454)
XLA Ops:
  62.9 13.2 collective-permute-done.3
  80.0 57.3 %collective-permute-done.4 = bf16[2,256,8,128]{3,1,2,0:T(8,128)(2,1)} collective-permute-done((bf16[2,256,8,128]{3,1,2,0:T(8,128)(2,1)}, bf16[2,256,8,128]{3,1,2,0:T(8,128)(2,1)}, u32[]{:S(2)}, u32[]{:S(2)}) %collective-permute-start.4) | collective-permute-done | bytes 1048608 | tf_op jit(solution)/shard_map/ppermute | solution.py:21
  142.2 46.6 %collective-permute-done.1 = bf16[2,256,8,128]{1,3,2,0:T(8,128)(2,1)} collective-permute-done((bf16[2,256,8,128]{1,3,2,0:T(8,128)(2,1)}, bf16[2,256,8,128]{1,3,2,0:T(8,128)(2,1)}, u32[]{:S(2)}, u32[]{:S(2)}) %collective-permute-start.1) | collective-permute-done | bytes 1048608 | tf_op jit(solution)/shard_map/ppermute | solution.py:21
  214.4 36.3 %all-gather.19.cloned.1.call-done = bf16[8,256,8,128]{3,2,1,0:T(8,128)(2,1)} async-done(((bf16[1,256,8,128]{3,2,1,0:T(8,128)(2,1)}), bf16[8,256,8,128]{3,2,1,0:T(8,128)(2,1)}) %all-gather.19.cloned.1.call-update) | async-done | bytes 4194320 | tf_op jit(solution)/shard_map/all_gather | solution.py:26
  254.7 69.9 %all-gather.21.cloned.1.call-done = bf16[8,256,8,128]{3,2,1,0:T(8,128)(2,1)} async-done(((bf16[1,256,8,128]{3,2,1,0:T(8,128)(2,1)}), bf16[8,256,8,128]{3,2,1,0:T(8,128)(2,1)}) %all-gather.21.cloned.1.call-update) | async-done | bytes 4194320 | tf_op jit(solution)/shard_map/all_gather | solution.py:26
  328.5 69.7 %all-gather.23.cloned.1.call-done = bf16[8,256,8,128]{3,2,1,0:T(8,128)(2,1)} async-done(((bf16[1,256,8,128]{3,2,1,0:T(8,128)(2,1)}), bf16[8,256,8,128]{3,2,1,0:T(8,128)(2,1)}) %all-gather.23.cloned.1.call-update) | async-done | bytes 4194320 | tf_op jit(solution)/shard_map/all_gather | solution.py:26
  402.2 69.8 %all-gather.25.cloned.1.call-done = bf16[8,256,8,128]{3,2,1,0:T(8,128)(2,1)} async-done(((bf16[1,256,8,128]{3,2,1,0:T(8,128)(2,1)}), bf16[8,256,8,128]{3,2,1,0:T(8,128)(2,1)}) %all-gather.25.cloned.1.call-update) | async-done | bytes 4194320 | tf_op jit(solution)/shard_map/all_gather | solution.py:26
  475.8 69.8 %all-gather.27.cloned.1.call-done = bf16[8,256,8,128]{3,2,1,0:T(8,128)(2,1)} async-done(((bf16[1,256,8,128]{3,2,1,0:T(8,128)(2,1)}), bf16[8,256,8,128]{3,2,1,0:T(8,128)(2,1)}) %all-gather.27.cloned.1.call-update) | async-done | bytes 4194320 | tf_op jit(solution)/shard_map/all_gather | solution.py:26
  549.5 69.9 %all-gather.29.cloned.1.call-done = bf16[8,256,8,128]{3,2,1,0:T(8,128)(2,1)} async-done(((bf16[1,256,8,128]{3,2,1,0:T(8,128)(2,1)}), bf16[8,256,8,128]{3,2,1,0:T(8,128)(2,1)}) %all-gather.29.cloned.1.call-update) | async-done | bytes 4194320 | tf_op jit(solution)/shard_map/all_gather | solution.py:26
  622.5 70.8 %all-gather.31.cloned.1.call-done = bf16[8,256,8,128]{3,2,1,0:T(8,128)(2,1)} async-done(((bf16[1,256,8,128]{3,2,1,0:T(8,128)(2,1)}), bf16[8,256,8,128]{3,2,1,0:T(8,128)(2,1)}) %all-gather.31.cloned.1.call-update) | async-done | bytes 4194320 | tf_op jit(solution)/shard_map/all_gather | solution.py:26
  698.0 15.4 fusion.43
  713.4 23.0 %copy.237 = f32[2,8,256,8,256]{2,4,3,1,0:T(8,128)} copy(f32[2,8,256,8,256]{2,4,0,3,1:T(8,128)} %get-tuple-element.111) | data formatting | bytes 67108864 | tf_op jit(solution)/shard_map/while/body/eval_jaxpr/jit(_where)/select_n | solution.py:65
  736.5 17.4 exponential_reduce_fusion
  753.9 27.4 %fusion.3 = bf16[2,8,256,3328]{2,3,1,0:T(8,128)(2,1)} fusion(f32[2,8,256,2048]{2,3,1,0:T(8,128)} %bitcast.268, f32[2,8,256,1280]{2,3,1,0:T(8,128)} %bitcast.271, f32[2,8,256]{2,1,0:T(8,128)S(1)} %log_add_fusion), kind=kLoop, calls=%fused_computation.7 | loop fusion | flops 40894464 | bytes 81805312 | tf_op jit(solution)/shard_map/while/body/eval_jaxpr/convert_element_type | solution.py:126
  781.2 14.2 slice.103
  808.5 32.2 %all-gather.35.cloned.1.call-done = bf16[8,256,8,128]{3,2,1,0:T(8,128)(2,1)} async-done(((bf16[1,256,8,128]{3,2,1,0:T(8,128)(2,1)}), bf16[8,256,8,128]{3,2,1,0:T(8,128)(2,1)}) %all-gather.35.cloned.1.call-update) | async-done | bytes 4194320 | tf_op jit(solution)/shard_map/all_gather | solution.py:26
  844.1 70.4 %all-gather.37.cloned.1.call-done = bf16[8,256,8,128]{3,2,1,0:T(8,128)(2,1)} async-done(((bf16[1,256,8,128]{3,2,1,0:T(8,128)(2,1)}), bf16[8,256,8,128]{3,2,1,0:T(8,128)(2,1)}) %all-gather.37.cloned.1.call-update) | async-done | bytes 4194320 | tf_op jit(solution)/shard_map/all_gather | solution.py:26
  918.7 69.5 %all-gather.39.cloned.1.call-done = bf16[8,256,8,128]{3,2,1,0:T(8,128)(2,1)} async-done(((bf16[1,256,8,128]{3,2,1,0:T(8,128)(2,1)}), bf16[8,256,8,128]{3,2,1,0:T(8,128)(2,1)}) %all-gather.39.cloned.1.call-update) | async-done | bytes 4194320 | tf_op jit(solution)/shard_map/all_gather | solution.py:26
  992.4 69.6 %all-gather.41.cloned.1.call-done = bf16[8,256,8,128]{3,2,1,0:T(8,128)(2,1)} async-done(((bf16[1,256,8,128]{3,2,1,0:T(8,128)(2,1)}), bf16[8,256,8,128]{3,2,1,0:T(8,128)(2,1)}) %all-gather.41.cloned.1.call-update) | async-done | bytes 4194320 | tf_op jit(solution)/shard_map/all_gather | solution.py:26
  1066.2 69.5 %all-gather.43.cloned.1.call-done = bf16[8,256,8,128]{3,2,1,0:T(8,128)(2,1)} async-done(((bf16[1,256,8,128]{3,2,1,0:T(8,128)(2,1)}), bf16[8,256,8,128]{3,2,1,0:T(8,128)(2,1)}) %all-gather.43.cloned.1.call-update) | async-done | bytes 4194320 | tf_op jit(solution)/shard_map/all_gather | solution.py:26
  1139.9 69.5 %all-gather.45.cloned.1.call-done = bf16[8,256,8,128]{3,2,1,0:T(8,128)(2,1)} async-done(((bf16[1,256,8,128]{3,2,1,0:T(8,128)(2,1)}), bf16[8,256,8,128]{3,2,1,0:T(8,128)(2,1)}) %all-gather.45.cloned.1.call-update) | async-done | bytes 4194320 | tf_op jit(solution)/shard_map/all_gather | solution.py:26
  1215.4 67.6 %all-gather.47.cloned.1.call-done = bf16[8,256,8,128]{3,2,1,0:T(8,128)(2,1)} async-done(((bf16[1,256,8,128]{3,2,1,0:T(8,128)(2,1)}), bf16[8,256,8,128]{3,2,1,0:T(8,128)(2,1)}) %all-gather.47.cloned.1.call-update) | async-done | bytes 4194320 | tf_op jit(solution)/shard_map/all_gather | solution.py:26
  1297.3 18.0 %convolution_bitcast_fusion = f32[2,8,256,8,256]{2,4,0,3,1:T(8,128)} fusion(bf16[8,256,8,128]{1,3,0,2:T(8,128)(2,1)} %bitcast_dynamic-update-slice_fusion.8, bf16[2,256,8,128,1]{3,2,1,0,4:T(8,128)(2,1)S(1)} %bitcast.294), kind=kOutput, calls=%fused_computation.11 | convolution fusion | flops 2147483648 | bytes 38797312 | tf_op jit(solution)/shard_map/while/body/eval_jaxpr/gqhd,nkhd->ghqnk/dot_general | solution.py:155
  1335.2 22.7 %copy.254 = f32[2,8,256,8,256]{2,4,3,1,0:T(8,128)} copy(f32[2,8,256,8,256]{2,4,0,3,1:T(8,128)} %convolution_bitcast_fusion) | data formatting | bytes 67108864 | tf_op jit(solution)/shard_map/while/body/eval_jaxpr/gqhd,nkhd->ghqnk/transpose | solution.py:155
  1358.0 43.4 %fusion.2 = bf16[2,8,256,3328]{2,3,1,0:T(8,128)(2,1)} fusion(f32[2,8,256,2048]{2,3,1,0:T(8,128)} %bitcast.275, f32[2,8,256,1280]{2,3,1,0:T(8,128)} %bitcast.278, f32[2,8,256,2048]{2,3,1,0:T(8,128)} %bitcast.269, f32[2,8,256,1280]{2,3,1,0:T(8,128)} %bitcast.272, f32[2,8,256]{2,1,0:T(8,128)S(1)} %bitcast.302, f32[2,8,256]{2,1,0:T(8,128)S(1)} %log_add_fusion), kind=kLoop, calls=%fused_computation.4 | loop fusion | flops 95420416 | bytes 136347648 | tf_op jit(solution)/shard_map/while/body/eval_jaxpr/convert_element_type | solution.py:162
  1401.3 14.0 slice.105
  1415.3 12.3 fusion.35
  1432.3 12.4 fusion.30
  1458.6 12.7 fusion.45
  1485.1 55.3 %reduce-scatter.3.cloned.1.call-done = bf16[8,32,8,128]{3,1,2,0:T(8,128)(2,1)} async-done(((bf16[8,256,8,128]{3,1,2,0:T(8,128)(2,1)}), bf16[8,32,8,128]{3,1,2,0:T(8,128)(2,1)}) %reduce-scatter.3.cloned.1.call-update) | async-done | bytes 524304 | tf_op jit(solution)/shard_map/reduce_scatter | solution.py:227
  1541.6 91.3 %reduce-scatter.5.cloned.1.call-done = bf16[8,32,8,128]{3,1,2,0:T(8,128)(2,1)} async-done(((bf16[8,256,8,128]{3,1,2,0:T(8,128)(2,1)}), bf16[8,32,8,128]{3,1,2,0:T(8,128)(2,1)}) %reduce-scatter.5.cloned.1.call-update) | async-done | bytes 524304 | tf_op jit(solution)/shard_map/reduce_scatter | solution.py:230
  1708.7 35.3 %collective-permute-done.8 = bf16[2,256,8,128]{3,1,2,0:T(8,128)(2,1)} collective-permute-done((bf16[2,256,8,128]{3,1,2,0:T(8,128)(2,1)}, bf16[2,256,8,128]{3,1,2,0:T(8,128)(2,1)}, u32[]{:S(2)}, u32[]{:S(2)}) %collective-permute-start.8) | collective-permute-done | bytes 1048608 | tf_op jit(solution)/shard_map/ppermute | solution.py:21
  (185 shorter events, 283.9 us)
Async XLA Ops:
  7.2 202.8 %all-gather.17.cloned.1.call-start = ((), (), s32[]{:S(2)}) async-start(), calls=%async_computation.4 | async-start | bytes 4718592 | tf_op jit(solution)/shard_map/all_gather | solution.py:26
  34.0 216.8 %all-gather.19.cloned.1.call-start = ((), (), s32[]{:S(2)}) async-start(), calls=%async_computation.5 | async-start | bytes 4718592 | tf_op jit(solution)/shard_map/all_gather | solution.py:26
  34.7 289.9 %all-gather.21.cloned.1.call-start = ((), (), s32[]{:S(2)}) async-start(), calls=%async_computation.6 | async-start | bytes 4718592 | tf_op jit(solution)/shard_map/all_gather | solution.py:26
  35.5 362.8 %all-gather.23.cloned.1.call-start = ((), (), s32[]{:S(2)}) async-start(), calls=%async_computation.7 | async-start | bytes 4718592 | tf_op jit(solution)/shard_map/all_gather | solution.py:26
  36.0 435.9 %all-gather.25.cloned.1.call-start = ((), (), s32[]{:S(2)}) async-start(), calls=%async_computation.8 | async-start | bytes 4718592 | tf_op jit(solution)/shard_map/all_gather | solution.py:26
  36.6 509.0 %all-gather.27.cloned.1.call-start = ((), (), s32[]{:S(2)}) async-start(), calls=%async_computation.9 | async-start | bytes 4718592 | tf_op jit(solution)/shard_map/all_gather | solution.py:26
  37.2 582.2 %all-gather.29.cloned.1.call-start = ((), (), s32[]{:S(2)}) async-start(), calls=%async_computation.10 | async-start | bytes 4718592 | tf_op jit(solution)/shard_map/all_gather | solution.py:26
  37.9 655.3 %all-gather.31.cloned.1.call-start = ((), (), s32[]{:S(2)}) async-start(), calls=%async_computation.11 | async-start | bytes 4718592 | tf_op jit(solution)/shard_map/all_gather | solution.py:26
  38.7 765.6 %all-gather.33.cloned.1.call-start = ((), (), s32[]{:S(2)}) async-start(), calls=%async_computation.12 | async-start | bytes 4718592 | tf_op jit(solution)/shard_map/all_gather | solution.py:26
  40.9 799.8 %all-gather.35.cloned.1.call-start = ((), (), s32[]{:S(2)}) async-start(), calls=%async_computation.13 | async-start | bytes 4718592 | tf_op jit(solution)/shard_map/all_gather | solution.py:26
  41.5 873.1 %all-gather.37.cloned.1.call-start = ((), (), s32[]{:S(2)}) async-start(), calls=%async_computation.14 | async-start | bytes 4718592 | tf_op jit(solution)/shard_map/all_gather | solution.py:26
  42.2 946.0 %all-gather.39.cloned.1.call-start = ((), (), s32[]{:S(2)}) async-start(), calls=%async_computation.15 | async-start | bytes 4718592 | tf_op jit(solution)/shard_map/all_gather | solution.py:26
  42.8 1019.3 %all-gather.41.cloned.1.call-start = ((), (), s32[]{:S(2)}) async-start(), calls=%async_computation.16 | async-start | bytes 4718592 | tf_op jit(solution)/shard_map/all_gather | solution.py:26
  43.5 1092.2 %all-gather.43.cloned.1.call-start = ((), (), s32[]{:S(2)}) async-start(), calls=%async_computation.17 | async-start | bytes 4718592 | tf_op jit(solution)/shard_map/all_gather | solution.py:26
  44.1 1165.3 %all-gather.45.cloned.1.call-start = ((), (), s32[]{:S(2)}) async-start(), calls=%async_computation.18 | async-start | bytes 4718592 | tf_op jit(solution)/shard_map/all_gather | solution.py:26
  44.7 1238.4 %all-gather.47.cloned.1.call-start = ((), (), s32[]{:S(2)}) async-start(), calls=%async_computation.19 | async-start | bytes 4718592 | tf_op jit(solution)/shard_map/all_gather | solution.py:26
  45.9 30.2 %collective-permute-start.3 = (bf16[2,256,8,128]{3,1,2,0:T(8,128)(2,1)}, bf16[2,256,8,128]{3,1,2,0:T(8,128)(2,1)}, u32[]{:S(2)}, u32[]{:S(2)}) collective-permute-start(bf16[2,256,8,128]{3,1,2,0:T(8,128)(2,1)} %copy.223), channel_id=1, source_target_pairs={{0,2},{2,0},{4,6},{6,4},{8,10},{10,8},{12,14},{14,12},{1,3},{3,1},... | collective-permute-start | bytes 3145736 | tf_op jit(solution)/shard_map/ppermute | solution.py:21
  48.9 88.4 %collective-permute-start.4 = (bf16[2,256,8,128]{3,1,2,0:T(8,128)(2,1)}, bf16[2,256,8,128]{3,1,2,0:T(8,128)(2,1)}, u32[]{:S(2)}, u32[]{:S(2)}) collective-permute-start(bf16[2,256,8,128]{3,1,2,0:T(8,128)(2,1)} %copy.223), channel_id=1, source_target_pairs={{0,4},{2,6},{4,0},{6,2},{8,12},{10,14},{12,8},{14,10},{1,5},{3,7},... | collective-permute-start | bytes 3145736 | tf_op jit(solution)/shard_map/ppermute | solution.py:21
  50.4 88.3 %collective-permute-start.5 = (bf16[2,256,8,128]{3,1,2,0:T(8,128)(2,1)}, bf16[2,256,8,128]{3,1,2,0:T(8,128)(2,1)}, u32[]{:S(2)}, u32[]{:S(2)}) collective-permute-start(bf16[2,256,8,128]{3,1,2,0:T(8,128)(2,1)} %copy.223), channel_id=1, source_target_pairs={{0,8},{2,10},{4,12},{6,14},{8,0},{10,2},{12,4},{14,6},{1,9},{3,11}... | collective-permute-start | bytes 3145736 | tf_op jit(solution)/shard_map/ppermute | solution.py:21
  54.5 85.6 %collective-permute-start = (bf16[2,256,8,128]{1,3,2,0:T(8,128)(2,1)}, bf16[2,256,8,128]{1,3,2,0:T(8,128)(2,1)}, u32[]{:S(2)}, u32[]{:S(2)}) collective-permute-start(bf16[2,256,8,128]{1,3,2,0:T(8,128)(2,1)} %copy.218), channel_id=1, source_target_pairs={{0,2},{2,0},{4,6},{6,4},{8,10},{10,8},{12,14},{14,12},{1,3},{3,1},... | collective-permute-start | bytes 3145736 | tf_op jit(solution)/shard_map/ppermute | solution.py:21
  55.0 133.8 %collective-permute-start.1 = (bf16[2,256,8,128]{1,3,2,0:T(8,128)(2,1)}, bf16[2,256,8,128]{1,3,2,0:T(8,128)(2,1)}, u32[]{:S(2)}, u32[]{:S(2)}) collective-permute-start(bf16[2,256,8,128]{1,3,2,0:T(8,128)(2,1)} %copy.218), channel_id=1, source_target_pairs={{0,4},{2,6},{4,0},{6,2},{8,12},{10,14},{12,8},{14,10},{1,5},{3,7},... | collective-permute-start | bytes 3145736 | tf_op jit(solution)/shard_map/ppermute | solution.py:21
  55.5 1484.9 %reduce-scatter.3.cloned.1.call-start = ((), (), s32[]{:S(2)}) async-start(), calls=%async_computation.20 | async-start | bytes 4718592 | tf_op jit(solution)/shard_map/reduce_scatter | solution.py:227
  76.1 122.7 %collective-permute-start.2 = (bf16[2,256,8,128]{1,3,2,0:T(8,128)(2,1)S(1)}, bf16[2,256,8,128]{1,3,2,0:T(8,128)(2,1)S(1)}, u32[]{:S(2)}, u32[]{:S(2)}) collective-permute-start(bf16[2,256,8,128]{1,3,2,0:T(8,128)(2,1)S(1)} %copy-done.12), channel_id=1, source_target_pairs={{0,8},{2,10},{4,12},{6,14},{8,0},{10,2},{12,4},{14,6},{1,9},{3,11}... | collective-permute-start | bytes 3145736 | tf_op jit(solution)/shard_map/ppermute | solution.py:21
  1432.3 200.6 %reduce-scatter.5.cloned.1.call-start = ((), (), s32[]{:S(2)}) async-start(), calls=%async_computation.21 | async-start | bytes 4718592 | tf_op jit(solution)/shard_map/reduce_scatter | solution.py:230
  1475.0 209.8 %collective-permute-start.10 = (bf16[2,256,8,128]{3,1,2,0:T(8,128)(2,1)}, bf16[2,256,8,128]{3,1,2,0:T(8,128)(2,1)}, u32[]{:S(2)}, u32[]{:S(2)}) collective-permute-start(bf16[2,256,8,128]{3,1,2,0:T(8,128)(2,1)} %get-tuple-element.50), channel_id=1, source_target_pairs={{0,4},{2,6},{4,0},{6,2},{8,12},{10,14},{12,8},{14,10},{1,5},{3,7},... | collective-permute-start | bytes 3145736 | tf_op jit(solution)/shard_map/ppermute | solution.py:21
  1475.7 218.1 %collective-permute-start.11 = (bf16[2,256,8,128]{3,1,2,0:T(8,128)(2,1)}, bf16[2,256,8,128]{3,1,2,0:T(8,128)(2,1)}, u32[]{:S(2)}, u32[]{:S(2)}) collective-permute-start(bf16[2,256,8,128]{3,1,2,0:T(8,128)(2,1)} %get-tuple-element.49), channel_id=1, source_target_pairs={{0,8},{2,10},{4,12},{6,14},{8,0},{10,2},{12,4},{14,6},{1,9},{3,11}... | collective-permute-start | bytes 3145736 | tf_op jit(solution)/shard_map/ppermute | solution.py:21
  1477.1 216.7 %collective-permute-start.9 = (bf16[2,256,8,128]{3,1,2,0:T(8,128)(2,1)}, bf16[2,256,8,128]{3,1,2,0:T(8,128)(2,1)}, u32[]{:S(2)}, u32[]{:S(2)}) collective-permute-start(bf16[2,256,8,128]{3,1,2,0:T(8,128)(2,1)} %get-tuple-element.48), channel_id=1, source_target_pairs={{0,2},{2,0},{4,6},{6,4},{8,10},{10,8},{12,14},{14,12},{1,3},{3,1},... | collective-permute-start | bytes 3145736 | tf_op jit(solution)/shard_map/ppermute | solution.py:21
  1638.1 30.6 %all-to-all-start.1 = ((bf16[16,32,8,128]{3,2,1,0:T(8,128)(2,1)}), bf16[16,32,8,128]{3,2,1,0:T(8,128)(2,1)}, u32[]{:S(2)}, u32[]{:S(2)}) async-start(bf16[16,32,8,128]{3,2,1,0:T(8,128)(2,1)} %get-tuple-element.46), calls=%async_computation.3 | async-start | bytes 2097152 | tf_op jit(solution)/shard_map/all_to_all | solution.py:246
  1646.2 62.4 %collective-permute-start.6 = (bf16[2,256,8,128]{3,1,2,0:T(8,128)(2,1)}, bf16[2,256,8,128]{3,1,2,0:T(8,128)(2,1)}, u32[]{:S(2)}, u32[]{:S(2)}) collective-permute-start(bf16[2,256,8,128]{3,1,2,0:T(8,128)(2,1)} %get-tuple-element.66), channel_id=1, source_target_pairs={{0,2},{2,0},{4,6},{6,4},{8,10},{10,8},{12,14},{14,12},{1,3},{3,1},... | collective-permute-start | bytes 3145736 | tf_op jit(solution)/shard_map/ppermute | solution.py:21
  1648.2 60.4 %collective-permute-start.7 = (bf16[2,256,8,128]{3,1,2,0:T(8,128)(2,1)}, bf16[2,256,8,128]{3,1,2,0:T(8,128)(2,1)}, u32[]{:S(2)}, u32[]{:S(2)}) collective-permute-start(bf16[2,256,8,128]{3,1,2,0:T(8,128)(2,1)} %get-tuple-element.68), channel_id=1, source_target_pairs={{0,4},{2,6},{4,0},{6,2},{8,12},{10,14},{12,8},{14,10},{1,5},{3,7},... | collective-permute-start | bytes 3145736 | tf_op jit(solution)/shard_map/ppermute | solution.py:21
  1668.6 38.2 %all-to-all-start = ((bf16[16,32,8,128]{3,2,1,0:T(8,128)(2,1)}), bf16[16,32,8,128]{3,2,1,0:T(8,128)(2,1)}, u32[]{:S(2)}, u32[]{:S(2)}) async-start(bf16[16,32,8,128]{3,2,1,0:T(8,128)(2,1)} %get-tuple-element.47), calls=%async_computation.1 | async-start | bytes 2097152 | tf_op jit(solution)/shard_map/all_to_all | solution.py:243
  1684.7 59.2 %collective-permute-start.8 = (bf16[2,256,8,128]{3,1,2,0:T(8,128)(2,1)}, bf16[2,256,8,128]{3,1,2,0:T(8,128)(2,1)}, u32[]{:S(2)}, u32[]{:S(2)}) collective-permute-start(bf16[2,256,8,128]{3,1,2,0:T(8,128)(2,1)} %get-tuple-element.67), channel_id=1, source_target_pairs={{0,8},{2,10},{4,12},{6,14},{8,0},{10,2},{12,4},{14,6},{1,9},{3,11}... | collective-permute-start | bytes 3145736 | tf_op jit(solution)/shard_map/ppermute | solution.py:21
  (15 other events, 345.1 us)
Sparse Core Ops, SparseCore 0:
  34.1 139.9 all-gather.16
  176.2 74.4 all-gather.18
  252.9 71.6 all-gather.20
  326.5 71.6 all-gather.22
  400.2 71.6 all-gather.24
  473.9 71.6 all-gather.26
  547.7 71.6 all-gather.28
  621.5 71.6 all-gather.30
  695.4 71.6 all-gather.32
  769.0 71.6 all-gather.34
  842.9 71.6 all-gather.36
  916.5 71.6 all-gather.38
  990.3 71.6 all-gather.40
  1064.0 71.6 all-gather.42
  1137.7 71.6 all-gather.44
  1211.4 71.6 all-gather.46
  1432.4 107.9 reduce-scatter.2
  1544.3 88.5 reduce-scatter.4
